TPU v7x, 32 devices: a whole 2x2x4 slice. The times are simulated.
32 devices in a mesh: row: 8 (over y, x, core), col: 4 (over z).
Axes of the slice: x: 2, y: 2, z: 4, core: 2. Of those that a mesh axis runs over, the one named last changes fastest.
Arguments:
- fixed_matrix_encodings: int32 [8192, 53248], P('row', 'col'), may hold values from 0 to 254, as said below
- line_restore_multiplier: float32 [8192], P('row'), may hold values from 0.001 to 0.01
- central_up_matrix: float32 [8192, 16], P('row', 'col'), may hold values from -1.5 to 1.5
- central_down_matrix: float32 [16, 53248], P('row', 'col'), may hold values from -1.5 to 1.5
- running_mean_up: float32 [8192, 16], P('row', 'col'), may hold values from -1.8 to 1.8
- squared_average_up: float32 [8192, 16], P('row', 'col'), may hold values from 0.05 to 0.5
- running_mean_down: float32 [16, 53248], P('row', 'col'), may hold values from -1.8 to 1.8
- squared_average_down: float32 [16, 53248], P('row', 'col'), may hold values from 0.05 to 0.5
- participant_change_up: bfloat16 [32, 8192, 16], P(('row', 'col')), may hold values from -48 to 48
- participant_change_down: bfloat16 [32, 16, 53248], P(('row', 'col')), may hold values from -48 to 48
- client_tallies: int32 [32, 2], P(('row', 'col')), may hold values from 1 to 64
Outputs:
- combined_normalized_entries: bfloat16 [8192, 53248], P('row', 'col')
- fresh_line_multipliers: float32 [8192], P('row')
- lora_b_next: float32 [8192, 16], P('row', 'col')
- lora_a_next: float32 [16, 53248], P('row', 'col')
- moment_b_next: float32 [8192, 16], P('row', 'col')
- second_b_next: float32 [8192, 16], P('row', 'col')
- moment_a_next: float32 [16, 53248], P('row', 'col')
- second_a_next: float32 [16, 53248], P('row', 'col')
Inputs may be any that keep to these rules, and one draw needn't show every extreme that they name: `fixed_matrix_encodings`: FP8 e4m3 bit patterns; the not-a-number patterns 127 and 255 never occur.
All inputs are finite; a program needn't handle non-finite values. Where the computation divides by a largest or mean magnitude, that divisor is 1e-20 or more.
Results may differ from a plain program's by a relative error of at most 0.0053.
Values may be sent and summed in bfloat16 or wider, within the bound.
A program may use at most 192 MiB of HBM per device.

v0:
```python
import functools

import jax
import jax.numpy as jnp
from jax import lax
from jax.experimental import pallas as pl
from jax.experimental.pallas import tpu as pltpu
from jax.sharding import PartitionSpec as P

first_decay = 0.9
second_decay = 0.99
server_rate = 0.1
adam_floor = 0.001
adapter_scale = 2.0
count_scale = 64.0
fp8_top = 448.0
peak_eps = 1e-06
MESH = pl.DeviceIdType.MESH
LANES = 128
decode_lines = 32
merge_lines = 128
code_slots = 3
stage_slots = 2


def tile_of(width, limit):
    best = LANES
    for tile in range(LANES, limit + 1, LANES):
        if width % tile == 0:
            best = tile
    return best


def adaptive_update(param, moment, second, grad):
    moment_next = first_decay * moment + (1.0 - first_decay) * grad
    second_next = second_decay * second + (1.0 - second_decay) * grad * grad
    param_next = param - server_rate * moment_next / (jnp.sqrt(second_next) + adam_floor)
    return (param_next, moment_next, second_next)


def scaled_decode(codes):
    low = codes & 127
    mantissa = codes & 7
    mantissa = jnp.where(low > 7, mantissa | 8, mantissa)
    magnitude = mantissa << jnp.maximum(low >> 3, 1)
    return jnp.where(codes > 127, -magnitude, magnitude).astype(jnp.float32)


def merge_kernel(
    rows_count, cols_count,
    codes, scale, pb, mb, vb, pa, ma, va, delta_b, delta_a, weight,
    merged, peak_wide, peak_out, nb, nmb, nvb, na, nma, nva,
    dense, code_buf, got_b, got_a, got_w, fac_b, fac_a, all_b, all_a, wide_b, wide_a,
    left, right, stage, scale_wide, top, top_send, got_top,
    code_sem, out_sem, send_sem, recv_sem, gather_send, gather_recv, own_sem,
):
    my_row, my_col = lax.axis_index("row"), lax.axis_index("col")
    count = rows_count * cols_count
    me = my_row * cols_count + my_col
    depth, width = dense.shape
    steps = depth // decode_lines
    tile = tile_of(width, 1024)
    tiles = width // tile
    rank_b, rank_a = pb.shape[0], pa.shape[0]

    def fetch(i):
        slot = lax.rem(i, code_slots)
        return pltpu.make_async_copy(
            codes.at[pl.ds(i * decode_lines, decode_lines)], code_buf.at[slot], code_sem.at[slot]
        )

    for i in range(code_slots):
        fetch(i).start()

    barrier = pltpu.get_barrier_semaphore()

    def greet(k, _):
        to = lax.rem(me + k, count)
        pl.semaphore_signal(
            barrier, inc=1, device_id=(to // cols_count, lax.rem(to, cols_count)), device_id_type=MESH
        )
        return 0

    lax.fori_loop(1, count, greet, 0)
    pl.semaphore_wait(barrier, count - 1)

    def block_a(row, col):
        return delta_a.at[row, :, pl.ds(pl.multiple_of(col * width, LANES), width)]

    def block_b(row, col):
        return delta_b.at[col, :, pl.ds(pl.multiple_of(row * depth, LANES), depth)]

    def exchange(to, source):
        row, col = to // cols_count, lax.rem(to, cols_count)
        parts = (
            (weight, got_w.at[source]),
            (block_b(row, col), got_b.at[source]),
            (block_a(row, col), got_a.at[source]),
        )
        return [
            pltpu.make_async_remote_copy(
                src_ref=src, dst_ref=dst, send_sem=send_sem.at[n, to], recv_sem=recv_sem.at[n, source],
                device_id=(row, col), device_id_type=MESH,
            )
            for n, (src, dst) in enumerate(parts)
        ]

    def send(k, _):
        for copy in exchange(lax.rem(me + k, count), me):
            copy.start()
        return 0

    lax.fori_loop(1, count, send, 0)
    own = [
        pltpu.make_async_copy(weight, got_w.at[me], own_sem.at[0]),
        pltpu.make_async_copy(block_b(my_row, my_col), got_b.at[me], own_sem.at[1]),
        pltpu.make_async_copy(block_a(my_row, my_col), got_a.at[me], own_sem.at[2]),
    ]
    for copy in own:
        copy.start()

    for b in range(depth // LANES):
        line = jnp.broadcast_to(scale[b : b + 1, :] * 2.0 ** (-10), (LANES, LANES))
        scale_wide[b * LANES : (b + 1) * LANES, :] = line.T

    def decode_step(i, _):
        slot = lax.rem(i, code_slots)
        fetch(i).wait()

        def column(j, _):
            at = pl.ds(pl.multiple_of(j * tile, LANES), tile)
            for g in range(decode_lines // 16):
                value = scaled_decode(code_buf[slot, g * 16 : (g + 1) * 16, at])
                dense[pl.ds(pl.multiple_of(i * decode_lines + g * 16, 16), 16), at] = value.astype(
                    jnp.bfloat16
                )
            return 0

        lax.fori_loop(0, tiles, column, 0)

        @pl.when(i + code_slots < steps)
        def _():
            fetch(i + code_slots).start()

        return 0

    lax.fori_loop(0, steps, decode_step, 0)

    for copy in own:
        copy.wait()

    def arrive(k, _):
        source = lax.rem(me + k, count)
        for copy in exchange(source, source):
            copy.wait_recv()
        return 0

    lax.fori_loop(1, count, arrive, 0)

    def summed(got, which, at, shape):
        def add(s, total):
            return total + got_w[s, which : which + 1, 0:1] * got[s, :, at].astype(jnp.float32)

        return lax.fori_loop(0, count, add, jnp.zeros(shape, jnp.float32), unroll=8)

    grad_b = summed(got_b, 0, slice(None), (rank_b, depth))
    p, m, v = adaptive_update(pb[...], mb[...], vb[...], grad_b)
    nb[...] = p
    nmb[...] = m
    nvb[...] = v
    fac_b[...] = p.astype(jnp.bfloat16)

    def gather_b(to, source):
        return pltpu.make_async_remote_copy(
            src_ref=fac_b, dst_ref=all_b.at[source], send_sem=gather_send.at[0, to],
            recv_sem=gather_recv.at[0, source], device_id=(my_row, to), device_id_type=MESH,
        )

    def gather_a(to, source):
        return pltpu.make_async_remote_copy(
            src_ref=fac_a, dst_ref=all_a.at[source], send_sem=gather_send.at[1, to],
            recv_sem=gather_recv.at[1, source], device_id=(to, my_col), device_id_type=MESH,
        )

    for k in range(1, cols_count):
        gather_b(lax.rem(my_col + k, cols_count), my_col).start()
    own_b = pltpu.make_async_copy(fac_b, all_b.at[my_col], own_sem.at[0])
    own_b.start()

    def update_a(j, _):
        at = pl.ds(pl.multiple_of(j * tile, LANES), tile)
        grad = summed(got_a, 1, at, (rank_a, tile))
        p, m, v = adaptive_update(pa[:, at], ma[:, at], va[:, at], grad)
        na[:, at] = p
        nma[:, at] = m
        nva[:, at] = v
        fac_a[:, at] = p.astype(jnp.bfloat16)
        return 0

    lax.fori_loop(0, tiles, update_a, 0)
    for k in range(1, rows_count):
        gather_a(lax.rem(my_row + k, rows_count), my_row).start()
    own_a = pltpu.make_async_copy(fac_a, all_a.at[my_row], own_sem.at[1])
    own_a.start()

    own_b.wait()
    for k in range(1, cols_count):
        source = lax.rem(my_col + k, cols_count)
        gather_b(source, source).wait_recv()
    for c in range(cols_count):
        wide_b[c * rank_b : (c + 1) * rank_b, :] = all_b[c].astype(jnp.float32)
    left[...] = wide_b[...].T.astype(jnp.bfloat16)

    own_a.wait()
    for k in range(1, rows_count):
        source = lax.rem(my_row + k, rows_count)
        gather_a(source, source).wait_recv()

    def assemble(j, _):
        at = pl.ds(pl.multiple_of(j * tile, LANES), tile)
        for r in range(rows_count):
            wide_a[r * rank_a : (r + 1) * rank_a, :] = all_a[r, :, at].astype(jnp.float32)
        right[:, at] = wide_a[...].astype(jnp.bfloat16)
        return 0

    lax.fori_loop(0, tiles, assemble, 0)

    def put(i):
        slot = lax.rem(i, stage_slots)
        lines = pl.ds(pl.multiple_of(i * merge_lines, merge_lines), merge_lines)
        return pltpu.make_async_copy(stage.at[slot], merged.at[lines], out_sem.at[slot])

    merge_steps = depth // merge_lines

    def merge_step(i, _):
        slot = lax.rem(i, stage_slots)
        lines = pl.ds(pl.multiple_of(i * merge_lines, merge_lines), merge_lines)

        @pl.when(i >= stage_slots)
        def _():
            put(i - stage_slots).wait()

        factor = left[lines, :]
        line_scale = scale_wide[lines, :]

        def column(j, highest):
            for t in range(tile // LANES):
                lane = pl.ds(pl.multiple_of(j * tile + t * LANES, LANES), LANES)
                product = jnp.dot(factor, right[:, lane], preferred_element_type=jnp.float32)
                value = dense[lines, lane].astype(jnp.float32) * line_scale
                value = value + adapter_scale * product
                highest = jnp.maximum(highest, jnp.abs(value))
                stage[slot, :, lane] = value.astype(jnp.bfloat16)
            return highest

        top[lines, :] = lax.fori_loop(
            0, tiles, column, jnp.zeros((merge_lines, LANES), jnp.float32)
        )
        put(i).start()
        return 0

    lax.fori_loop(0, merge_steps, merge_step, 0)

    for b in range(depth // LANES):
        square = top[b * LANES : (b + 1) * LANES, :]
        top_send[b : b + 1, :] = jnp.max(square.T, axis=0, keepdims=True)

    def gather_top(to, source):
        return pltpu.make_async_remote_copy(
            src_ref=top_send, dst_ref=got_top.at[source], send_sem=gather_send.at[2, to],
            recv_sem=gather_recv.at[2, source], device_id=(my_row, to), device_id_type=MESH,
        )

    for k in range(1, cols_count):
        gather_top(lax.rem(my_col + k, cols_count), my_col).start()
    peak = top_send[...]
    for k in range(1, cols_count):
        source = lax.rem(my_col + k, cols_count)
        gather_top(source, source).wait_recv()
        peak = jnp.maximum(peak, got_top[source])
    peak = peak + peak_eps
    peak_out[...] = peak / fp8_top
    for b in range(depth // LANES):
        peak_wide[b * LANES : (b + 1) * LANES, :] = jnp.broadcast_to(
            1.0 / peak[b : b + 1, :], (LANES, LANES)
        ).T

    def drain(i, _):
        put(i).wait()
        return 0

    lax.fori_loop(merge_steps - stage_slots, merge_steps, drain, 0)

    def sent(k, _):
        for copy in exchange(lax.rem(me + k, count), me):
            copy.wait_send()
        return 0

    lax.fori_loop(1, count, sent, 0)
    for k in range(1, cols_count):
        to = lax.rem(my_col + k, cols_count)
        gather_b(to, my_col).wait_send()
        gather_top(to, my_col).wait_send()
    for k in range(1, rows_count):
        gather_a(lax.rem(my_row + k, rows_count), my_row).wait_send()


def normalize_kernel(merged, inverse, out):
    for t in range(merged.shape[1] // LANES):
        at = slice(t * LANES, (t + 1) * LANES)
        out[:, at] = (merged[:, at].astype(jnp.float32) * inverse[...]).astype(jnp.bfloat16)


def local(
    fixed_matrix_encodings,
    line_restore_multiplier,
    central_up_matrix,
    central_down_matrix,
    running_mean_up,
    squared_average_up,
    running_mean_down,
    squared_average_down,
    participant_change_up,
    participant_change_down,
    client_tallies,
):
    rows_count = lax.axis_size("row")
    cols_count = lax.axis_size("col")
    count = rows_count * cols_count
    depth, width = fixed_matrix_encodings.shape
    rank_b = central_up_matrix.shape[1]
    rank_a = central_down_matrix.shape[0]
    rank = participant_change_down.shape[1]
    blocks = depth // LANES
    everyone = client_tallies.shape[0] * count
    weights = client_tallies.astype(jnp.float32) / (count_scale * everyone)
    weight = jnp.broadcast_to(weights[0][:, None], (2, LANES))
    delta_b = participant_change_up[0].T.reshape(cols_count, rank_b, depth * rows_count)
    delta_a = participant_change_down[0].reshape(rows_count, rank_a, width * cols_count)
    anywhere = pl.BlockSpec(memory_space=pl.ANY)
    vmem = pl.BlockSpec(memory_space=pltpu.VMEM)
    f32, bf16 = jnp.float32, jnp.bfloat16
    shape = jax.ShapeDtypeStruct
    outs = pl.pallas_call(
        functools.partial(merge_kernel, rows_count, cols_count),
        out_shape=[
            shape((depth, width), bf16),
            shape((depth, LANES), f32),
            shape((blocks, LANES), f32),
        ]
        + [shape((rank_b, depth), f32)] * 3
        + [shape((rank_a, width), f32)] * 3,
        in_specs=[anywhere] + [vmem] * 7 + [anywhere] * 2 + [vmem],
        out_specs=[anywhere] + [vmem] * 8,
        scratch_shapes=[
            pltpu.VMEM((depth, width), bf16),
            pltpu.VMEM((code_slots, decode_lines, width), jnp.int32),
            pltpu.VMEM((count, rank_b, depth), bf16),
            pltpu.VMEM((count, rank_a, width), bf16),
            pltpu.VMEM((count, 2, LANES), f32),
            pltpu.VMEM((rank_b, depth), bf16),
            pltpu.VMEM((rank_a, width), bf16),
            pltpu.VMEM((cols_count, rank_b, depth), bf16),
            pltpu.VMEM((rows_count, rank_a, width), bf16),
            pltpu.VMEM((rank, depth), f32),
            pltpu.VMEM((rank, tile_of(width, 1024)), f32),
            pltpu.VMEM((depth, rank), bf16),
            pltpu.VMEM((rank, width), bf16),
            pltpu.VMEM((stage_slots, merge_lines, width), bf16),
            pltpu.VMEM((depth, LANES), f32),
            pltpu.VMEM((depth, LANES), f32),
            pltpu.VMEM((blocks, LANES), f32),
            pltpu.VMEM((cols_count, blocks, LANES), f32),
            pltpu.SemaphoreType.DMA((code_slots,)),
            pltpu.SemaphoreType.DMA((stage_slots,)),
            pltpu.SemaphoreType.DMA((3, count)),
            pltpu.SemaphoreType.DMA((3, count)),
            pltpu.SemaphoreType.DMA((3, max(rows_count, cols_count))),
            pltpu.SemaphoreType.DMA((3, max(rows_count, cols_count))),
            pltpu.SemaphoreType.DMA((3,)),
        ],
        compiler_params=pltpu.CompilerParams(
            collective_id=0, has_side_effects=True, vmem_limit_bytes=62_000_000
        ),
    )(
        fixed_matrix_encodings,
        line_restore_multiplier.reshape(blocks, LANES),
        central_up_matrix.T,
        running_mean_up.T,
        squared_average_up.T,
        central_down_matrix,
        running_mean_down,
        squared_average_down,
        delta_b,
        delta_a,
        weight,
    )
    merged, inverse, fresh, nb, nmb, nvb, na, nma, nva = outs
    step = 64
    normalized = pl.pallas_call(
        normalize_kernel,
        grid=(depth // step,),
        out_shape=shape((depth, width), bf16),
        in_specs=[
            pl.BlockSpec((step, width), lambda i: (i, 0)),
            pl.BlockSpec((step, LANES), lambda i: (i, 0)),
        ],
        out_specs=pl.BlockSpec((step, width), lambda i: (i, 0)),
    )(merged, inverse)
    return (normalized, fresh.reshape(depth), nb.T, na, nmb.T, nvb.T, nma, nva)


def solution(mesh):
    grid = P("row", "col")
    clients = P(("row", "col"), None, None)
    return jax.shard_map(
        local,
        mesh=mesh,
        in_specs=(grid, P("row"), grid, grid, grid, grid, grid, grid, clients, clients, P(("row", "col"), None)),
        out_specs=(grid, P("row"), grid, grid, grid, grid, grid, grid),
        check_vma=False,
    )
```

profile of v0, /device:TPU:0, one launch (start us, length us, event | category | flops | bytes accessed | tf_op | source)
XLA Modules:
  0.0 133.1 jit_solution(17779879150215597517)
XLA Ops:
  0.6 0.7 multiply_bitcast_fusion
  1.3 0.6 broadcast_in_dim.8.weight
  1.9 1.8 %reshape.27.delta_b = bf16[4,4,8192]{2,1,0:T(4,128)(2,1)} reshape(bf16[16,8192]{1,0:T(8,128)(2,1)} %bitcast.13) | data formatting | bytes 524288 | tf_op jit(solution)/shard_map/reshape | solution.py:338
  3.7 3.1 %reshape_squeeze.3.delta_a = bf16[8,2,53248]{2,1,0:T(2,128)(2,1)} reshape(bf16[1,16,53248]{2,1,0:T(8,128)(2,1)} %param.20) | data formatting | bytes 3407872 | tf_op jit(solution)/shard_map/reshape;squeeze | solution.py:339
  6.8 96.4 %shard_map.170 = (bf16[1024,13312]{1,0:T(8,128)(2,1)}, f32[1024,128]{1,0:T(8,128)}, f32[8,128]{1,0:T(8,128)}, f32[4,1024]{1,0:T(4,128)}, f32[4,1024]{1,0:T(4,128...) custom-call(s32[1024,13312]{1,0:T(8,128)} %codes.1, f32[8,128]{1,0:T(8,128)} %bitcast.20, ...), custom_call_target="tpu_custom_call" | custom-call | tf_op jit(solution)/shard_map/pallas_call | solution.py:344
  103.2 0.0 copy-start.6
  103.2 0.0 copy-start.5
  103.2 0.0 copy-start.2
  103.3 0.0 copy-start.4
  103.3 0.0 copy-start.3
  103.3 0.0 copy-start.1
  103.3 0.0 copy-start
  103.3 25.4 %shard_map.171 = bf16[1024,13312]{1,0:T(8,128)(2,1)} custom-call(bf16[1024,13312]{1,0:T(8,128)(2,1)} %get-tuple-element.17.merged, f32[1024,128]{1,0:T(8,128)} %get-tuple-element.18.inverse), custom_call_target="tpu_custom_call" | custom-call | tf_op jit(solution)/shard_map/pallas_call | solution.py:400
  128.7 0.0 copy-done.6
  128.7 0.6 copy.26
  129.3 0.0 copy-done.5
  129.3 0.6 copy.27
  129.9 0.0 copy-done.2
  129.9 0.6 copy.28
  130.6 0.0 copy-done.4
  130.6 0.6 copy.29
  131.2 0.0 copy-done.3
  131.2 0.6 copy.30
  131.8 0.0 copy-done.1
  131.8 0.6 copy.31
  132.4 0.0 copy-done
  132.4 0.6 copy.32
Async XLA Ops:
  103.2 25.5 %copy-start.6 = (f32[8,128]{1,0:T(8,128)S(1)}, f32[8,128]{1,0:T(8,128)}, u32[]{:S(2)}) copy-start(f32[8,128]{1,0:T(8,128)} %get-tuple-element.19) | copy-start | bytes 12292
  103.2 26.1 %copy-start.5 = (f32[4,1024]{1,0:T(4,128)S(1)}, f32[4,1024]{1,0:T(4,128)}, u32[]{:S(2)}) copy-start(f32[4,1024]{1,0:T(4,128)} %get-tuple-element.20) | copy-start | bytes 49156
  103.2 26.7 %copy-start.2 = (f32[2,13312]{1,0:T(2,128)S(1)}, f32[2,13312]{1,0:T(2,128)}, u32[]{:S(2)}) copy-start(f32[2,13312]{1,0:T(2,128)} %get-tuple-element.37) | copy-start | bytes 319492
  103.3 27.3 %copy-start.4 = (f32[4,1024]{1,0:T(4,128)S(1)}, f32[4,1024]{1,0:T(4,128)}, u32[]{:S(2)}) copy-start(f32[4,1024]{1,0:T(4,128)} %get-tuple-element.22) | copy-start | bytes 49156
  103.3 27.9 %copy-start.3 = (f32[4,1024]{1,0:T(4,128)S(1)}, f32[4,1024]{1,0:T(4,128)}, u32[]{:S(2)}) copy-start(f32[4,1024]{1,0:T(4,128)} %get-tuple-element.23) | copy-start | bytes 49156
  103.3 28.5 %copy-start.1 = (f32[2,13312]{1,0:T(2,128)S(1)}, f32[2,13312]{1,0:T(2,128)}, u32[]{:S(2)}) copy-start(f32[2,13312]{1,0:T(2,128)} %get-tuple-element.40) | copy-start | bytes 319492
  103.3 29.2 %copy-start = (f32[2,13312]{1,0:T(2,128)S(1)}, f32[2,13312]{1,0:T(2,128)}, u32[]{:S(2)}) copy-start(f32[2,13312]{1,0:T(2,128)} %get-tuple-element.41) | copy-start | bytes 319492
where the time goes:
time: 134 us; the launch traced here: 133 us
  Pallas kernels  122 us (91%)
  local copies, waits for them, and re-layouts  9.9 us (7%)
    pallas_call x1, Pallas kernels, local(): pl.pallas_call(functools.partial(merge_kernel, rows_count, cols_count), o...  96.4 us
    pallas_call x1, Pallas kernels, local(): pl.pallas_call(normalize_kernel, grid=(depth // step,), out_shape=shape((...  25.4 us
    unnamed x21, local copies, waits for them, and re-layouts  4.37 us
    another operation x1, local copies, waits for them, and re-layouts, local(): participant_change_down[0].reshape(rows_count, rank_a, width * cols_count)  3.14 us

commit v1 on v0

--- a/solution.py
+++ b/solution.py
@@ -21,6 +21,12 @@
 merge_lines = 128
 code_slots = 3
 stage_slots = 2
+fetch_lines = 64
+fetch_slots = 3
+pass_lines = 128
+out_lines = 64
+out_slots = 3
+decode_plan = (3, 1, 1, 1, 2, 1, 1, 1, 1, 2, 2)
 
 
 def tile_of(width, limit):
@@ -311,7 +317,7 @@
         out[:, at] = (merged[:, at].astype(jnp.float32) * inverse[...]).astype(jnp.bfloat16)
 
 
-def local(
+def direct_local(
     fixed_matrix_encodings,
     line_restore_multiplier,
     central_up_matrix,
@@ -410,6 +416,568 @@
     return (normalized, fresh.reshape(depth), nb.T, na, nmb.T, nvb.T, nma, nva)
 
 
+def packed_decode(codes):
+    half = jnp.bfloat16
+    value = codes.astype(jnp.float32).astype(half)
+    negative = value > half(127)
+    value = jnp.where(negative, value - half(128), value)
+    power = jnp.maximum(jnp.floor(value * half(0.125)) - half(1), half(0))
+    value = value - power * half(8)
+    return jnp.where(negative, -value, value) * jnp.exp2(power)
+
+
+def staged_kernel(
+    rows_count, cols_count, everyone,
+    tallies, codes, scale, pb, mb, vb, pa, ma, va, delta_b, delta_a,
+    dense, inverse, fresh, nb, nmb, nvb, na, nma, nva,
+    code_buf, weight, got_w, mine_a, core_a, pair_a, chip_a, line_a, got_a, sum_a,
+    mine_b, core_b, pair_b, chip_b, line_b, got_b,
+    state_a, back_a, wide_a, fac_a, right, fac_b, all_b, wide_b, left, top, top_send, got_top,
+    code_sem, own_sem, core_send, core_recv, chip_send, chip_recv, line_send, line_recv,
+    state_send, state_recv, back_send, back_recv, row_send, row_recv, col_send, col_recv,
+):
+    my_row, my_col = lax.axis_index("row"), lax.axis_index("col")
+    chips = rows_count // 2
+    core, chip = lax.rem(my_row, 2), my_row // 2
+    depth, width = dense.shape
+    rank = delta_a.shape[0]
+    rank_b, rank_a = pb.shape[0], pa.shape[0]
+    part = width // rows_count
+    half = chips * part
+    slot_of = core * chips + chip
+    tile = tile_of(width, 1024)
+    f32, bf16 = jnp.float32, jnp.bfloat16
+    partner = (chip * 2 + 1 - core, my_col)
+
+    def remote(src, dst, send, recv, to):
+        return pltpu.make_async_remote_copy(
+            src_ref=src, dst_ref=dst, send_sem=send, recv_sem=recv, device_id=to, device_id_type=MESH
+        )
+
+    def lanes(start, size):
+        return pl.ds(pl.multiple_of(start, LANES), size)
+
+    def fetch(i):
+        slot = lax.rem(i, fetch_slots)
+        return pltpu.make_async_copy(
+            codes.at[pl.ds(i * fetch_lines, fetch_lines)], code_buf.at[slot], code_sem.at[slot]
+        )
+
+    steps = depth // fetch_lines
+    for i in range(fetch_slots):
+        fetch(i).start()
+
+    def own_copies():
+        copies = []
+        for c in range(cols_count):
+            copies.append((delta_a.at[:, lanes(c * width + core * half, half)], mine_a.at[c]))
+        for q in range(chips):
+            copies.append((delta_b.at[:, lanes((2 * q + core) * depth, depth)], mine_b.at[q]))
+        for n, state in enumerate((pa, ma, va)):
+            copies.append((state.at[:, lanes(slot_of * part, part)], state_a.at[n, my_row]))
+        return [pltpu.make_async_copy(s, d, own_sem.at[n]) for n, (s, d) in enumerate(copies)]
+
+    own = own_copies()
+    for copy in own:
+        copy.start()
+
+    for n in range(2):
+        portion = tallies[0, n].astype(f32) / (count_scale * everyone)
+        weight[n * 8 : (n + 1) * 8, :] = jnp.full((8, LANES), portion, f32)
+
+    barrier = pltpu.get_barrier_semaphore()
+    for k in range(1, rows_count):
+        pl.semaphore_signal(
+            barrier, inc=1, device_id=(lax.rem(my_row + k, rows_count), my_col), device_id_type=MESH
+        )
+    for k in range(1, cols_count):
+        pl.semaphore_signal(
+            barrier, inc=1, device_id=(my_row, lax.rem(my_col + k, cols_count)), device_id_type=MESH
+        )
+    pl.semaphore_wait(barrier, rows_count + cols_count - 2)
+
+    def core_copy_a(c):
+        return remote(
+            delta_a.at[:, lanes(c * width + (1 - core) * half, half)], core_a.at[c],
+            core_send.at[c], core_recv.at[c], partner,
+        )
+
+    def core_copy_b(q):
+        return remote(
+            delta_b.at[:, lanes((2 * q + 1 - core) * depth, depth)], core_b.at[q],
+            core_send.at[cols_count + q], core_recv.at[cols_count + q], partner,
+        )
+
+    last = cols_count + chips
+    core_copy_w = remote(weight, got_w, core_send.at[last], core_recv.at[last], partner)
+
+    def state_copy(n, to, source):
+        piece = lax.rem(to, 2) * chips + to // 2
+        return remote(
+            (pa, ma, va)[n].at[:, lanes(piece * part, part)], state_a.at[n, source],
+            state_send.at[n, to], state_recv.at[n, source], (to, my_col),
+        )
+
+    core_copy_w.start()
+    for k in range(1, cols_count + 1):
+        core_copy_a(lax.rem(my_col + k, cols_count)).start()
+    for q in range(chips):
+        core_copy_b(q).start()
+    for k in range(1, rows_count):
+        for n in range(3):
+            state_copy(n, lax.rem(my_row + k, rows_count), my_row).start()
+
+    def decode_step(i, _):
+        slot = lax.rem(i, fetch_slots)
+        fetch(i).wait()
+
+        def column(j, _):
+            at = lanes(j * tile, tile)
+            for g in range(fetch_lines // 16):
+                dense[pl.ds(pl.multiple_of(i * fetch_lines + g * 16, 16), 16), at] = packed_decode(
+                    code_buf[slot, g * 16 : (g + 1) * 16, at]
+                )
+            return 0
+
+        lax.fori_loop(0, width // tile, column, 0)
+
+        @pl.when(i + fetch_slots < steps)
+        def _():
+            fetch(i + fetch_slots).start()
+
+        return 0
+
+    done = [0]
+    plan = list(decode_plan)
+
+    def decode_some():
+        until = min(steps, done[0] + plan.pop(0)) if plan else steps
+        if until > done[0]:
+            lax.fori_loop(done[0], until, decode_step, 0)
+        done[0] = until
+
+    decode_some()
+
+    for copy in own:
+        copy.wait()
+    core_copy_w.wait_recv()
+
+    def blend(mine, theirs, which):
+        ours = weight[which * 8 : which * 8 + 1, 0:1] * mine.astype(f32)
+        return (ours + got_w[which * 8 : which * 8 + 1, 0:1] * theirs.astype(f32)).astype(bf16)
+
+    def chip_copy_a(q, c, source):
+        return remote(
+            pair_a.at[q, c], chip_a.at[source, c], chip_send.at[q, c], chip_recv.at[source, c],
+            (q * 2 + core, my_col),
+        )
+
+    def chip_copy_b(q, source):
+        return remote(
+            pair_b.at[q], chip_b.at[source], chip_send.at[q, cols_count],
+            chip_recv.at[source, cols_count], (q * 2 + core, my_col),
+        )
+
+    for q in range(chips):
+        core_copy_b(q).wait_recv()
+    for q in range(chips):
+        pair_b[q] = blend(mine_b[q], core_b[q], 0)
+    for k in range(1, chips):
+        chip_copy_b(lax.rem(chip + k, chips), chip).start()
+    for k in range(1, cols_count + 1):
+        c = lax.rem(my_col + k, cols_count)
+        core_copy_a(c).wait_recv()
+        for q in range(chips):
+            at = slice(q * part, (q + 1) * part)
+            pair_a[q, c] = blend(mine_a[c, :, at], core_a[c, :, at], 1)
+        for j in range(1, chips):
+            chip_copy_a(lax.rem(chip + j, chips), c, chip).start()
+        decode_some()
+
+    def line_copy_a(c, source):
+        return remote(
+            line_a.at[c], got_a.at[source], line_send.at[0, c], line_recv.at[0, source], (my_row, c)
+        )
+
+    def line_copy_b(c, source):
+        return remote(
+            line_b.at[c], got_b.at[source], line_send.at[1, c], line_recv.at[1, source], (my_row, c)
+        )
+
+    total = pair_b[chip].astype(f32)
+    for k in range(1, chips):
+        source = lax.rem(chip + k, chips)
+        chip_copy_b(source, source).wait_recv()
+        total = total + chip_b[source].astype(f32)
+    for c in range(cols_count):
+        line_b[c] = total[c * rank_b : (c + 1) * rank_b, :]
+    for k in range(1, cols_count):
+        line_copy_b(lax.rem(my_col + k, cols_count), my_col).start()
+
+    for k in range(1, cols_count + 1):
+        c = lax.rem(my_col + k, cols_count)
+        total = pair_a[chip, c].astype(f32)
+        for j in range(1, chips):
+            source = lax.rem(chip + j, chips)
+            chip_copy_a(source, c, source).wait_recv()
+            total = total + chip_a[source, c].astype(f32)
+        if k < cols_count:
+            line_a[c] = total.astype(bf16)
+            line_copy_a(c, my_col).start()
+            decode_some()
+        else:
+            sum_a[...] = total
+
+    decode_some()
+
+    grad = line_b[my_col]
+    for k in range(1, cols_count):
+        source = lax.rem(my_col + k, cols_count)
+        line_copy_b(source, source).wait_recv()
+        grad = grad + got_b[source]
+    p, m, v = adaptive_update(pb[...], mb[...], vb[...], grad)
+    nb[...] = p
+    nmb[...] = m
+    nvb[...] = v
+    fac_b[...] = p.astype(bf16)
+
+    def gather_b(to, source):
+        return remote(
+            fac_b, all_b.at[source], col_send.at[0, to], col_recv.at[0, source], (my_row, to)
+        )
+
+    for k in range(1, cols_count):
+        gather_b(lax.rem(my_col + k, cols_count), my_col).start()
+
+    for k in range(1, rows_count):
+        for n in range(3):
+            source = lax.rem(my_row + k, rows_count)
+            state_copy(n, source, source).wait_recv()
+    for k in range(1, cols_count):
+        source = lax.rem(my_col + k, cols_count)
+        line_copy_a(source, source).wait_recv()
+
+    grad = sum_a[...]
+    for k in range(1, cols_count):
+        grad = grad + got_a[lax.rem(my_col + k, cols_count)].astype(f32)
+    for r in range(rows_count):
+        at = slice(r * rank_a, (r + 1) * rank_a)
+        p, m, v = adaptive_update(state_a[0, r], state_a[1, r], state_a[2, r], grad[at, :])
+        back_a[0, r] = p
+        back_a[1, r] = m
+        back_a[2, r] = v
+        wide_a[at, :] = p
+    fac_a[...] = wide_a[...].astype(bf16)
+
+    def right_at(row):
+        piece = lax.rem(row, 2) * chips + row // 2
+        return right.at[0:rank, lanes(piece * part, part)]
+
+    def gather_a(to, source):
+        return remote(
+            fac_a, right_at(source), row_send.at[to], row_recv.at[source], (to, my_col)
+        )
+
+    def back_copy(n, to, source):
+        piece = lax.rem(source, 2) * chips + source // 2
+        return remote(
+            back_a.at[n, to], (na, nma, nva)[n].at[:, lanes(piece * part, part)],
+            back_send.at[n, to], back_recv.at[n, source], (to, my_col),
+        )
+
+    for k in range(1, rows_count):
+        gather_a(lax.rem(my_row + k, rows_count), my_row).start()
+    own_right = pltpu.make_async_copy(fac_a, right_at(my_row), own_sem.at[0])
+    own_right.start()
+    own_factor = pltpu.make_async_copy(fac_b, all_b.at[my_col], own_sem.at[1])
+    own_factor.start()
+    own_back = [
+        pltpu.make_async_copy(
+            back_a.at[n, my_row], ref.at[:, lanes(slot_of * part, part)], own_sem.at[2 + n]
+        )
+        for n, ref in enumerate((na, nma, nva))
+    ]
+    for copy in own_back:
+        copy.start()
+    for k in range(1, rows_count):
+        for n in range(3):
+            back_copy(n, lax.rem(my_row + k, rows_count), my_row).start()
+
+    plan[:] = []
+    decode_some()
+
+    own_factor.wait()
+    for k in range(1, cols_count):
+        source = lax.rem(my_col + k, cols_count)
+        gather_b(source, source).wait_recv()
+    for c in range(cols_count):
+        wide_b[c * rank_b : (c + 1) * rank_b, :] = all_b[c].astype(f32)
+    for b in range(depth // LANES):
+        at = slice(b * LANES, (b + 1) * LANES)
+        folded = wide_b[0:rank, at] * (adapter_scale * 2.0**9 / scale[b : b + 1, :])
+        high = folded.astype(bf16).astype(f32)
+        wide_b[0:rank, at] = high
+        wide_b[rank : 2 * rank, at] = folded - high
+    left[...] = wide_b[...].T.astype(bf16)
+
+    own_right.wait()
+    for k in range(1, rows_count):
+        source = lax.rem(my_row + k, rows_count)
+        gather_a(source, source).wait_recv()
+
+    def repeat(j, _):
+        at = lanes(j * tile, tile)
+        right[rank : 2 * rank, at] = right[0:rank, at]
+        return 0
+
+    lax.fori_loop(0, width // tile, repeat, 0)
+
+    def merge_step(i, _):
+        lines = pl.ds(pl.multiple_of(i * pass_lines, pass_lines), pass_lines)
+        factor = left[lines, :]
+
+        def column(j, highest):
+            for t in range(tile // LANES):
+                lane = lanes(j * tile + t * LANES, LANES)
+                value = jnp.dot(factor, right[:, lane], preferred_element_type=f32)
+                value = value + dense[lines, lane].astype(f32)
+                highest = jnp.maximum(highest, jnp.abs(value))
+                dense[lines, lane] = value.astype(bf16)
+            return highest
+
+        top[lines, :] = lax.fori_loop(
+            0, width // tile, column, jnp.zeros((pass_lines, LANES), f32)
+        )
+        return 0
+
+    lax.fori_loop(0, depth // pass_lines, merge_step, 0)
+
+    for b in range(depth // LANES):
+        square = top[b * LANES : (b + 1) * LANES, :]
+        top_send[b : b + 1, :] = jnp.max(square.T, axis=0, keepdims=True)
+
+    def gather_top(to, source):
+        return remote(
+            top_send, got_top.at[source], col_send.at[1, to], col_recv.at[1, source], (my_row, to)
+        )
+
+    for k in range(1, cols_count):
+        gather_top(lax.rem(my_col + k, cols_count), my_col).start()
+    peak = top_send[...]
+    for k in range(1, cols_count):
+        source = lax.rem(my_col + k, cols_count)
+        gather_top(source, source).wait_recv()
+        peak = jnp.maximum(peak, got_top[source])
+    unit = scale[...] * 2.0 ** (-9)
+    peak = peak * unit + peak_eps
+    fresh[...] = peak / fp8_top
+    ratio = unit / peak
+    for b in range(depth // LANES):
+        inverse[b * LANES : (b + 1) * LANES, :] = jnp.broadcast_to(
+            ratio[b : b + 1, :], (LANES, LANES)
+        ).T
+
+    for copy in own_back:
+        copy.wait()
+    core_copy_w.wait_send()
+    for c in range(cols_count):
+        core_copy_a(c).wait_send()
+    for q in range(chips):
+        core_copy_b(q).wait_send()
+    for k in range(1, chips):
+        q = lax.rem(chip + k, chips)
+        chip_copy_b(q, chip).wait_send()
+        for c in range(cols_count):
+            chip_copy_a(q, c, chip).wait_send()
+    for k in range(1, cols_count):
+        to = lax.rem(my_col + k, cols_count)
+        line_copy_a(to, my_col).wait_send()
+        line_copy_b(to, my_col).wait_send()
+        gather_b(to, my_col).wait_send()
+        gather_top(to, my_col).wait_send()
+    for k in range(1, rows_count):
+        to = lax.rem(my_row + k, rows_count)
+        gather_a(to, my_row).wait_send()
+        for n in range(3):
+            state_copy(n, to, my_row).wait_send()
+            back_copy(n, to, to).wait_recv()
+            back_copy(n, to, my_row).wait_send()
+
+
+def finish_kernel(small, merged, inverse, *refs):
+    ins, out, outs = refs[:small], refs[small], refs[small + 1 : 2 * small + 1]
+    stage, out_sem, small_sem = refs[2 * small + 1 :]
+    depth, width = merged.shape
+    tile = tile_of(width, 1024)
+    copies = [
+        pltpu.make_async_copy(src, dst, small_sem.at[n]) for n, (src, dst) in enumerate(zip(ins, outs))
+    ]
+    for copy in copies:
+        copy.start()
+
+    def put(i):
+        slot = lax.rem(i, out_slots)
+        return pltpu.make_async_copy(
+            stage.at[slot], out.at[pl.ds(pl.multiple_of(i * out_lines, out_lines), out_lines)], out_sem.at[slot]
+        )
+
+    steps = depth // out_lines
+
+    def step(i, _):
+        slot = lax.rem(i, out_slots)
+
+        @pl.when(i >= out_slots)
+        def _():
+            put(i - out_slots).wait()
+
+        lines = pl.ds(pl.multiple_of(i * out_lines, out_lines), out_lines)
+        factor = inverse[lines, :]
+
+        def column(j, _):
+            for t in range(tile // LANES):
+                at = pl.ds(pl.multiple_of(j * tile + t * LANES, LANES), LANES)
+                stage[slot, :, at] = (merged[lines, at].astype(jnp.float32) * factor).astype(jnp.bfloat16)
+            return 0
+
+        lax.fori_loop(0, width // tile, column, 0)
+        put(i).start()
+        return 0
+
+    lax.fori_loop(0, steps, step, 0)
+
+    def drain(i, _):
+        put(i).wait()
+        return 0
+
+    lax.fori_loop(steps - out_slots, steps, drain, 0)
+    for copy in copies:
+        copy.wait()
+
+
+def staged_local(
+    fixed_matrix_encodings,
+    line_restore_multiplier,
+    central_up_matrix,
+    central_down_matrix,
+    running_mean_up,
+    squared_average_up,
+    running_mean_down,
+    squared_average_down,
+    participant_change_up,
+    participant_change_down,
+    client_tallies,
+):
+    rows_count = lax.axis_size("row")
+    cols_count = lax.axis_size("col")
+    count = rows_count * cols_count
+    depth, width = fixed_matrix_encodings.shape
+    rank_b = central_up_matrix.shape[1]
+    rank_a = central_down_matrix.shape[0]
+    rank = participant_change_down.shape[1]
+    blocks = depth // LANES
+    chips = rows_count // 2
+    part = width // rows_count
+    half = chips * part
+    everyone = client_tallies.shape[0] * count
+    anywhere = pl.BlockSpec(memory_space=pl.ANY)
+    vmem = pl.BlockSpec(memory_space=pltpu.VMEM)
+    f32, bf16 = jnp.float32, jnp.bfloat16
+    here = pltpu.VMEM
+    dma = pltpu.SemaphoreType.DMA
+    small_shapes = [(blocks, LANES)] + [(rank_b, depth)] * 3 + [(rank_a, width)] * 3
+    outs = pl.pallas_call(
+        functools.partial(staged_kernel, rows_count, cols_count, everyone),
+        out_shape=[here((depth, width), bf16), here((depth, LANES), f32)]
+        + [here(shape, f32) for shape in small_shapes],
+        in_specs=[pl.BlockSpec(memory_space=pltpu.SMEM), anywhere] + [vmem] * 7 + [anywhere] * 2,
+        out_specs=[vmem] * 9,
+        scratch_shapes=[
+            here((fetch_slots, fetch_lines, width), jnp.int32),
+            here((16, LANES), f32),
+            here((16, LANES), f32),
+            here((cols_count, rank, half), bf16),
+            here((cols_count, rank, half), bf16),
+            here((chips, cols_count, rank, part), bf16),
+            here((chips, cols_count, rank, part), bf16),
+            here((cols_count, rank, part), bf16),
+            here((cols_count, rank, part), bf16),
+            here((rank, part), f32),
+            here((chips, rank, depth), bf16),
+            here((chips, rank, depth), bf16),
+            here((chips, rank, depth), bf16),
+            here((chips, rank, depth), bf16),
+            here((cols_count, rank_b, depth), f32),
+            here((cols_count, rank_b, depth), f32),
+            here((3, rows_count, rank_a, part), f32),
+            here((3, rows_count, rank_a, part), f32),
+            here((rank, part), f32),
+            here((rank, part), bf16),
+            here((2 * rank, width), bf16),
+            here((rank_b, depth), bf16),
+            here((cols_count, rank_b, depth), bf16),
+            here((2 * rank, depth), f32),
+            here((depth, 2 * rank), bf16),
+            here((depth, LANES), f32),
+            here((blocks, LANES), f32),
+            here((cols_count, blocks, LANES), f32),
+            dma((fetch_slots,)),
+            dma((cols_count + chips + 5,)),
+            dma((cols_count + chips + 1,)),
+            dma((cols_count + chips + 1,)),
+            dma((chips, cols_count + 1)),
+            dma((chips, cols_count + 1)),
+            dma((2, cols_count)),
+            dma((2, cols_count)),
+            dma((3, rows_count)),
+            dma((3, rows_count)),
+            dma((3, rows_count)),
+            dma((3, rows_count)),
+            dma((rows_count,)),
+            dma((rows_count,)),
+            dma((2, cols_count)),
+            dma((2, cols_count)),
+        ],
+        compiler_params=pltpu.CompilerParams(
+            collective_id=0, has_side_effects=True, vmem_limit_bytes=30_000_000
+        ),
+    )(
+        client_tallies,
+        fixed_matrix_encodings,
+        line_restore_multiplier.reshape(blocks, LANES),
+        central_up_matrix.T,
+        running_mean_up.T,
+        squared_average_up.T,
+        central_down_matrix,
+        running_mean_down,
+        squared_average_down,
+        participant_change_up[0].T,
+        participant_change_down[0],
+    )
+    small = len(small_shapes)
+    outs = [pltpu.with_memory_space_constraint(out, pltpu.VMEM) for out in outs]
+    normalized, fresh, nb, nmb, nvb, na, nma, nva = pl.pallas_call(
+        functools.partial(finish_kernel, small),
+        out_shape=[jax.ShapeDtypeStruct((depth, width), bf16)]
+        + [jax.ShapeDtypeStruct(shape, f32) for shape in small_shapes],
+        in_specs=[vmem] * (2 + small),
+        out_specs=[anywhere] * (1 + small),
+        scratch_shapes=[
+            here((out_slots, out_lines, width), bf16),
+            dma((out_slots,)),
+            dma((small,)),
+        ],
+        compiler_params=pltpu.CompilerParams(vmem_limit_bytes=30_000_000),
+    )(*outs)
+    return (normalized, fresh.reshape(depth), nb.T, na, nmb.T, nvb.T, nma, nva)
+
+
+def local(*args):
+    rows_count, width = lax.axis_size("row"), args[0].shape[1]
+    if rows_count % 2 == 0 and width % (rows_count * LANES) == 0:
+        return staged_local(*args)
+    return direct_local(*args)
+
+
 def solution(mesh):
     grid = P("row", "col")
     clients = P(("row", "col"), None, None)

time: 134 us -> 79.7 us (0.59)
  Pallas kernels: 122 us -> 78.9 us
  local copies, waits for them, and re-layouts: 9.9 us -> 0 us
    pallas_call x2, Pallas kernels: 122 us -> 78.9 us  [the longest x1 65.8 us: staged_local(): pl.pallas_call(functools.partial(staged_kernel, rows_count, cols_count, e...]
    unnamed x21 -> x0, local copies, waits for them, and re-layouts: 4.37 us -> none
    another operation x1 -> x0, local copies, waits for them, and re-layouts: 3.14 us -> none  [local(): participant_change_down[0].reshape(rows_count, rank_a, width * cols_count)]
    reshape x1 -> x0, local copies, waits for them, and re-layouts: 1.76 us -> none  [local(): participant_change_up[0].T.reshape(cols_count, rank_b, depth * rows_count)]
where the time goes in v1:
time: 79.7 us; the launch traced here: 79.6 us
  Pallas kernels  78.9 us (99%)
    pallas_call x1, Pallas kernels, staged_local(): pl.pallas_call(functools.partial(staged_kernel, rows_count, cols_count, e...  65.8 us
    pallas_call x1, Pallas kernels, staged_local(): pl.pallas_call(functools.partial(finish_kernel, small), out_shape=[jax.Sh...  13.2 us

profile of v1, /device:TPU:0, one launch (start us, length us, event | category | flops | bytes accessed | tf_op | source)
XLA Modules:
  0.0 79.6 jit_solution(12567052977576811776)
XLA Ops:
  0.6 65.8 %shard_map.170 = (bf16[1024,13312]{1,0:T(8,128)(2,1)S(1)}, f32[1024,128]{1,0:T(8,128)S(1)}, f32[8,128]{1,0:T(8,128)S(1)}, f32[4,1024]{1,0:T(4,128)S(1)}, f32[4,1...) custom-call(s32[1,2]{1,0:T(1,128)} %tallies.1, ...), custom_call_target="tpu_custom_call" | custom-call | tf_op jit(solution)/shard_map/pallas_call | solution.py:888
  66.4 13.2 %shard_map.171 = (bf16[1024,13312]{1,0:T(8,128)(2,1)}, f32[8,128]{1,0:T(8,128)}, f32[4,1024]{1,0:T(4,128)}, f32[4,1024]{1,0:T(4,128)}, f32[4,1024]{1,0:T(4,128)}...) custom-call(bf16[1024,13312]{1,0:T(8,128)(2,1)S(1)} %get-tuple-element.25.merged, ...), custom_call_target="tpu_custom_call" | custom-call | tf_op jit(solution)/shard_map/pallas_call | solution.py:958

commit v2 on v1

--- a/solution.py
+++ b/solution.py
@@ -23,10 +23,13 @@
 stage_slots = 2
 fetch_lines = 64
 fetch_slots = 3
-pass_lines = 128
+decode_group = 32
+decode_width = 1664
+pass_width = 512
+pass_lines = 32
 out_lines = 64
 out_slots = 3
-decode_plan = (3, 1, 1, 1, 2, 1, 1, 1, 1, 2, 2)
+decode_plan = (1, 0, 0, 0, 3, 2, 2, 2, 1)
 
 
 def tile_of(width, limit):
@@ -418,19 +421,20 @@
 
 def packed_decode(codes):
     half = jnp.bfloat16
-    value = codes.astype(jnp.float32).astype(half)
-    negative = value > half(127)
-    value = jnp.where(negative, value - half(128), value)
-    power = jnp.maximum(jnp.floor(value * half(0.125)) - half(1), half(0))
-    value = value - power * half(8)
-    return jnp.where(negative, -value, value) * jnp.exp2(power)
+    value = codes.astype(jnp.float32).astype(half) * half(0.125)
+    negative = value > half(15.9)
+    value = jnp.where(negative, value - half(16), value)
+    power = jnp.floor(jnp.maximum(value, half(1)))
+    value = (value - power) + half(1)
+    value = jnp.where(negative, -value, value)
+    return (value * jnp.exp2(power - half(7))).astype(jnp.float8_e4m3fn)
 
 
 def staged_kernel(
     rows_count, cols_count, everyone,
     tallies, codes, scale, pb, mb, vb, pa, ma, va, delta_b, delta_a,
-    dense, inverse, fresh, nb, nmb, nvb, na, nma, nva,
-    code_buf, weight, got_w, mine_a, core_a, pair_a, chip_a, line_a, got_a, sum_a,
+    merged, inverse, fresh, nb, nmb, nvb, na, nma, nva,
+    dense, code_buf, weight, got_w, mine_a, core_a, pair_a, chip_a, line_a, got_a, sum_a,
     mine_b, core_b, pair_b, chip_b, line_b, got_b,
     state_a, back_a, wide_a, fac_a, right, fac_b, all_b, wide_b, left, top, top_send, got_top,
     code_sem, own_sem, core_send, core_recv, chip_send, chip_recv, line_send, line_recv,
@@ -445,7 +449,7 @@
     part = width // rows_count
     half = chips * part
     slot_of = core * chips + chip
-    tile = tile_of(width, 1024)
+    tile = tile_of(width, decode_width)
     f32, bf16 = jnp.float32, jnp.bfloat16
     partner = (chip * 2 + 1 - core, my_col)
 
@@ -521,8 +525,9 @@
     core_copy_w.start()
     for k in range(1, cols_count + 1):
         core_copy_a(lax.rem(my_col + k, cols_count)).start()
-    for q in range(chips):
-        core_copy_b(q).start()
+        if k == 1:
+            for q in range(chips):
+                core_copy_b(q).start()
     for k in range(1, rows_count):
         for n in range(3):
             state_copy(n, lax.rem(my_row + k, rows_count), my_row).start()
@@ -533,9 +538,10 @@
 
         def column(j, _):
             at = lanes(j * tile, tile)
-            for g in range(fetch_lines // 16):
-                dense[pl.ds(pl.multiple_of(i * fetch_lines + g * 16, 16), 16), at] = packed_decode(
-                    code_buf[slot, g * 16 : (g + 1) * 16, at]
+            for g in range(fetch_lines // decode_group):
+                start = pl.multiple_of(i * fetch_lines + g * decode_group, decode_group)
+                dense[pl.ds(start, decode_group), at] = packed_decode(
+                    code_buf[slot, g * decode_group : (g + 1) * decode_group, at]
                 )
             return 0
 
@@ -578,12 +584,6 @@
             chip_recv.at[source, cols_count], (q * 2 + core, my_col),
         )
 
-    for q in range(chips):
-        core_copy_b(q).wait_recv()
-    for q in range(chips):
-        pair_b[q] = blend(mine_b[q], core_b[q], 0)
-    for k in range(1, chips):
-        chip_copy_b(lax.rem(chip + k, chips), chip).start()
     for k in range(1, cols_count + 1):
         c = lax.rem(my_col + k, cols_count)
         core_copy_a(c).wait_recv()
@@ -592,6 +592,12 @@
             pair_a[q, c] = blend(mine_a[c, :, at], core_a[c, :, at], 1)
         for j in range(1, chips):
             chip_copy_a(lax.rem(chip + j, chips), c, chip).start()
+        if k == 1:
+            for q in range(chips):
+                core_copy_b(q).wait_recv()
+                pair_b[q] = blend(mine_b[q], core_b[q], 0)
+            for j in range(1, chips):
+                chip_copy_b(lax.rem(chip + j, chips), chip).start()
         decode_some()
 
     def line_copy_a(c, source):
@@ -604,15 +610,16 @@
             line_b.at[c], got_b.at[source], line_send.at[1, c], line_recv.at[1, source], (my_row, c)
         )
 
-    total = pair_b[chip].astype(f32)
-    for k in range(1, chips):
-        source = lax.rem(chip + k, chips)
-        chip_copy_b(source, source).wait_recv()
-        total = total + chip_b[source].astype(f32)
-    for c in range(cols_count):
-        line_b[c] = total[c * rank_b : (c + 1) * rank_b, :]
-    for k in range(1, cols_count):
-        line_copy_b(lax.rem(my_col + k, cols_count), my_col).start()
+    def sum_b():
+        total = pair_b[chip].astype(f32)
+        for k in range(1, chips):
+            source = lax.rem(chip + k, chips)
+            chip_copy_b(source, source).wait_recv()
+            total = total + chip_b[source].astype(f32)
+        for c in range(cols_count):
+            line_b[c] = total[c * rank_b : (c + 1) * rank_b, :]
+        for k in range(1, cols_count):
+            line_copy_b(lax.rem(my_col + k, cols_count), my_col).start()
 
     for k in range(1, cols_count + 1):
         c = lax.rem(my_col + k, cols_count)
@@ -624,6 +631,8 @@
         if k < cols_count:
             line_a[c] = total.astype(bf16)
             line_copy_a(c, my_col).start()
+            if k == 1:
+                sum_b()
             decode_some()
         else:
             sum_a[...] = total
@@ -685,8 +694,10 @@
             back_send.at[n, to], back_recv.at[n, source], (to, my_col),
         )
 
-    for k in range(1, rows_count):
-        gather_a(lax.rem(my_row + k, rows_count), my_row).start()
+    for j in range(1, chips):
+        gather_a(lax.rem(chip + j, chips) * 2 + core, my_row).start()
+    for j in range(chips):
+        gather_a(lax.rem(chip + j, chips) * 2 + 1 - core, my_row).start()
     own_right = pltpu.make_async_copy(fac_a, right_at(my_row), own_sem.at[0])
     own_right.start()
     own_factor = pltpu.make_async_copy(fac_b, all_b.at[my_col], own_sem.at[1])
@@ -699,9 +710,6 @@
     ]
     for copy in own_back:
         copy.start()
-    for k in range(1, rows_count):
-        for n in range(3):
-            back_copy(n, lax.rem(my_row + k, rows_count), my_row).start()
 
     plan[:] = []
     decode_some()
@@ -714,43 +722,63 @@
         wide_b[c * rank_b : (c + 1) * rank_b, :] = all_b[c].astype(f32)
     for b in range(depth // LANES):
         at = slice(b * LANES, (b + 1) * LANES)
-        folded = wide_b[0:rank, at] * (adapter_scale * 2.0**9 / scale[b : b + 1, :])
+        folded = wide_b[0:rank, at] * (adapter_scale / scale[b : b + 1, :])
         high = folded.astype(bf16).astype(f32)
         wide_b[0:rank, at] = high
         wide_b[rank : 2 * rank, at] = folded - high
     left[...] = wide_b[...].T.astype(bf16)
 
+    top[...] = jnp.zeros((depth, LANES), f32)
+
+    def merge_tile(at, size):
+        for lines in range(0, depth, 1024):
+            deep = min(1024, depth - lines)
+            product = jnp.dot(
+                left[lines : lines + deep, :], right[:, lanes(at, size)], preferred_element_type=f32
+            )
+            for g in range(0, deep, pass_lines):
+                here = slice(lines + g, lines + g + pass_lines)
+                highest = top[here, :]
+                for t in range(0, size, LANES):
+                    lane = lanes(at + t, LANES)
+                    value = product[g : g + pass_lines, t : t + LANES] + dense[here, lane].astype(f32)
+                    highest = jnp.maximum(highest, jnp.abs(value))
+                    merged[here, lane] = value.astype(bf16)
+                top[here, :] = highest
+
+    def merge_piece(row):
+        start = (lax.rem(row, 2) * chips + row // 2) * part
+        at = lanes(start, part)
+        right[rank : 2 * rank, at] = right[0:rank, at]
+        whole = part // pass_width
+
+        def column(j, _):
+            merge_tile(start + j * pass_width, pass_width)
+            return 0
+
+        lax.fori_loop(0, whole, column, 0)
+        if part % pass_width:
+            merge_tile(start + whole * pass_width, part % pass_width)
+
+    def merge_from(row):
+        gather_a(row, row).wait_recv()
+        merge_piece(row)
+
+    def near(j, _):
+        merge_from(lax.rem(chip + j, chips) * 2 + core)
+        return 0
+
+    def far(j, _):
+        merge_from(lax.rem(chip + j, chips) * 2 + 1 - core)
+        return 0
+
     own_right.wait()
+    merge_piece(my_row)
+    lax.fori_loop(1, chips, near, 0)
     for k in range(1, rows_count):
-        source = lax.rem(my_row + k, rows_count)
-        gather_a(source, source).wait_recv()
-
-    def repeat(j, _):
-        at = lanes(j * tile, tile)
-        right[rank : 2 * rank, at] = right[0:rank, at]
-        return 0
-
-    lax.fori_loop(0, width // tile, repeat, 0)
-
-    def merge_step(i, _):
-        lines = pl.ds(pl.multiple_of(i * pass_lines, pass_lines), pass_lines)
-        factor = left[lines, :]
-
-        def column(j, highest):
-            for t in range(tile // LANES):
-                lane = lanes(j * tile + t * LANES, LANES)
-                value = jnp.dot(factor, right[:, lane], preferred_element_type=f32)
-                value = value + dense[lines, lane].astype(f32)
-                highest = jnp.maximum(highest, jnp.abs(value))
-                dense[lines, lane] = value.astype(bf16)
-            return highest
-
-        top[lines, :] = lax.fori_loop(
-            0, width // tile, column, jnp.zeros((pass_lines, LANES), f32)
-        )
-        return 0
-
-    lax.fori_loop(0, depth // pass_lines, merge_step, 0)
+        for n in range(3):
+            back_copy(n, lax.rem(my_row + k, rows_count), my_row).start()
+    lax.fori_loop(0, chips, far, 0)
 
     for b in range(depth // LANES):
         square = top[b * LANES : (b + 1) * LANES, :]
@@ -768,10 +796,9 @@
         source = lax.rem(my_col + k, cols_count)
         gather_top(source, source).wait_recv()
         peak = jnp.maximum(peak, got_top[source])
-    unit = scale[...] * 2.0 ** (-9)
-    peak = peak * unit + peak_eps
+    peak = peak * scale[...] + peak_eps
     fresh[...] = peak / fp8_top
-    ratio = unit / peak
+    ratio = scale[...] / peak
     for b in range(depth // LANES):
         inverse[b * LANES : (b + 1) * LANES, :] = jnp.broadcast_to(
             ratio[b : b + 1, :], (LANES, LANES)
@@ -892,6 +919,7 @@
         in_specs=[pl.BlockSpec(memory_space=pltpu.SMEM), anywhere] + [vmem] * 7 + [anywhere] * 2,
         out_specs=[vmem] * 9,
         scratch_shapes=[
+            here((depth, width), jnp.float8_e4m3fn),
             here((fetch_slots, fetch_lines, width), jnp.int32),
             here((16, LANES), f32),
             here((16, LANES), f32),
@@ -938,7 +966,7 @@
             dma((2, cols_count)),
         ],
         compiler_params=pltpu.CompilerParams(
-            collective_id=0, has_side_effects=True, vmem_limit_bytes=30_000_000
+            collective_id=0, has_side_effects=True, vmem_limit_bytes=38_000_000
         ),
     )(
         client_tallies,
@@ -966,7 +994,7 @@
             dma((out_slots,)),
             dma((small,)),
         ],
-        compiler_params=pltpu.CompilerParams(vmem_limit_bytes=30_000_000),
+        compiler_params=pltpu.CompilerParams(vmem_limit_bytes=38_000_000),
     )(*outs)
     return (normalized, fresh.reshape(depth), nb.T, na, nmb.T, nvb.T, nma, nva)
 

time: 79.7 us -> 64.6 us (0.81)
  Pallas kernels: 78.9 us -> 63.7 us
    pallas_call x1, Pallas kernels: 65.8 us -> 50.6 us  [staged_local(): pl.pallas_call(functools.partial(staged_kernel, rows_count, cols_count, e...]
where the time goes in v2:
time: 64.6 us; the launch traced here: 64.4 us
  Pallas kernels  63.7 us (99%)
  between operations  0.65 us (1%)
    pallas_call x1, Pallas kernels, staged_local(): pl.pallas_call(functools.partial(staged_kernel, rows_count, cols_count, e...  50.6 us
    pallas_call x1, Pallas kernels, staged_local(): pl.pallas_call(functools.partial(finish_kernel, small), out_shape=[jax.Sh...  13.2 us

profile of v2, /device:TPU:0, one launch (start us, length us, event | category | flops | bytes accessed | tf_op | source)
XLA Modules:
  0.0 64.4 jit_solution(4352262554977085743)
XLA Ops:
  0.6 50.6 %shard_map.170 = (bf16[1024,13312]{1,0:T(8,128)(2,1)S(1)}, f32[1024,128]{1,0:T(8,128)S(1)}, f32[8,128]{1,0:T(8,128)S(1)}, f32[4,1024]{1,0:T(4,128)S(1)}, f32[4,1...) custom-call(s32[1,2]{1,0:T(1,128)} %tallies.1, ...), custom_call_target="tpu_custom_call" | custom-call | tf_op jit(solution)/shard_map/pallas_call | solution.py:915
  51.2 13.2 %shard_map.171 = (bf16[1024,13312]{1,0:T(8,128)(2,1)}, f32[8,128]{1,0:T(8,128)}, f32[4,1024]{1,0:T(4,128)}, f32[4,1024]{1,0:T(4,128)}, f32[4,1024]{1,0:T(4,128)}...) custom-call(bf16[1024,13312]{1,0:T(8,128)(2,1)S(1)} %get-tuple-element.25.merged, ...), custom_call_target="tpu_custom_call" | custom-call | tf_op jit(solution)/shard_map/pallas_call | solution.py:986

commit v3 on v2

--- a/solution.py
+++ b/solution.py
@@ -29,7 +29,7 @@
 pass_lines = 32
 out_lines = 64
 out_slots = 3
-decode_plan = (1, 0, 0, 0, 3, 2, 2, 2, 1)
+decode_plan = (2, 0, 0, 0, 8, 4, 4, 4, 4)
 
 
 def tile_of(width, limit):
@@ -532,12 +532,19 @@
         for n in range(3):
             state_copy(n, lax.rem(my_row + k, rows_count), my_row).start()
 
-    def decode_step(i, _):
+    splits = 2 if width // tile % 2 == 0 else 1
+    share = width // tile // splits
+
+    def decode_step(unit, _):
+        i, turn = unit // splits, lax.rem(unit, splits)
         slot = lax.rem(i, fetch_slots)
-        fetch(i).wait()
+
+        @pl.when(turn == 0)
+        def _():
+            fetch(i).wait()
 
         def column(j, _):
-            at = lanes(j * tile, tile)
+            at = lanes((turn * share + j) * tile, tile)
             for g in range(fetch_lines // decode_group):
                 start = pl.multiple_of(i * fetch_lines + g * decode_group, decode_group)
                 dense[pl.ds(start, decode_group), at] = packed_decode(
@@ -545,9 +552,9 @@
                 )
             return 0
 
-        lax.fori_loop(0, width // tile, column, 0)
-
-        @pl.when(i + fetch_slots < steps)
+        lax.fori_loop(0, share, column, 0)
+
+        @pl.when((i + fetch_slots < steps) & (turn == splits - 1))
         def _():
             fetch(i + fetch_slots).start()
 
@@ -555,9 +562,10 @@
 
     done = [0]
     plan = list(decode_plan)
+    units = steps * splits
 
     def decode_some():
-        until = min(steps, done[0] + plan.pop(0)) if plan else steps
+        until = min(units, done[0] + plan.pop(0)) if plan else units
         if until > done[0]:
             lax.fori_loop(done[0], until, decode_step, 0)
         done[0] = until
@@ -746,39 +754,40 @@
                     merged[here, lane] = value.astype(bf16)
                 top[here, :] = highest
 
-    def merge_piece(row):
-        start = (lax.rem(row, 2) * chips + row // 2) * part
-        at = lanes(start, part)
+    def merge_piece(start, size):
+        at = lanes(start, size)
         right[rank : 2 * rank, at] = right[0:rank, at]
-        whole = part // pass_width
+        whole = size // pass_width
 
         def column(j, _):
             merge_tile(start + j * pass_width, pass_width)
             return 0
 
         lax.fori_loop(0, whole, column, 0)
-        if part % pass_width:
-            merge_tile(start + whole * pass_width, part % pass_width)
+        if size % pass_width:
+            merge_tile(start + whole * pass_width, size % pass_width)
 
     def merge_from(row):
         gather_a(row, row).wait_recv()
-        merge_piece(row)
+        merge_piece((lax.rem(row, 2) * chips + row // 2) * part, part)
 
     def near(j, _):
         merge_from(lax.rem(chip + j, chips) * 2 + core)
         return 0
 
     def far(j, _):
-        merge_from(lax.rem(chip + j, chips) * 2 + 1 - core)
+        source = lax.rem(chip + j, chips) * 2 + 1 - core
+        gather_a(source, source).wait_recv()
         return 0
 
     own_right.wait()
-    merge_piece(my_row)
+    merge_piece(slot_of * part, part)
     lax.fori_loop(1, chips, near, 0)
     for k in range(1, rows_count):
         for n in range(3):
             back_copy(n, lax.rem(my_row + k, rows_count), my_row).start()
     lax.fori_loop(0, chips, far, 0)
+    merge_piece((1 - core) * half, half)
 
     for b in range(depth // LANES):
         square = top[b * LANES : (b + 1) * LANES, :]
@@ -835,7 +844,7 @@
     ins, out, outs = refs[:small], refs[small], refs[small + 1 : 2 * small + 1]
     stage, out_sem, small_sem = refs[2 * small + 1 :]
     depth, width = merged.shape
-    tile = tile_of(width, 1024)
+    tile = tile_of(width, decode_width)
     copies = [
         pltpu.make_async_copy(src, dst, small_sem.at[n]) for n, (src, dst) in enumerate(zip(ins, outs))
     ]
@@ -857,13 +866,13 @@
         def _():
             put(i - out_slots).wait()
 
-        lines = pl.ds(pl.multiple_of(i * out_lines, out_lines), out_lines)
-        factor = inverse[lines, :]
-
         def column(j, _):
-            for t in range(tile // LANES):
-                at = pl.ds(pl.multiple_of(j * tile + t * LANES, LANES), LANES)
-                stage[slot, :, at] = (merged[lines, at].astype(jnp.float32) * factor).astype(jnp.bfloat16)
+            at = pl.ds(pl.multiple_of(j * tile, LANES), tile)
+            for g in range(0, out_lines, 16):
+                lines = pl.ds(pl.multiple_of(i * out_lines + g, 16), 16)
+                factor = jnp.tile(inverse[lines, :], (1, tile // LANES))
+                value = merged[lines, at].astype(jnp.float32) * factor
+                stage[slot, g : g + 16, at] = value.astype(jnp.bfloat16)
             return 0
 
         lax.fori_loop(0, width // tile, column, 0)
@@ -916,7 +925,7 @@
         functools.partial(staged_kernel, rows_count, cols_count, everyone),
         out_shape=[here((depth, width), bf16), here((depth, LANES), f32)]
         + [here(shape, f32) for shape in small_shapes],
-        in_specs=[pl.BlockSpec(memory_space=pltpu.SMEM), anywhere] + [vmem] * 7 + [anywhere] * 2,
+        in_specs=[pl.BlockSpec(memory_space=pltpu.SMEM), anywhere] + [vmem] * 4 + [anywhere] * 5,
         out_specs=[vmem] * 9,
         scratch_shapes=[
             here((depth, width), jnp.float8_e4m3fn),

time: 64.6 us -> 58.9 us (0.912)
  Pallas kernels: 63.7 us -> 58 us
    pallas_call x1, Pallas kernels: 13.2 us -> 9.49 us  [staged_local(): pl.pallas_call(functools.partial(finish_kernel, small), out_shape=[jax.Sh...]
    pallas_call x1, Pallas kernels: 50.6 us -> 48.5 us  [staged_local(): pl.pallas_call(functools.partial(staged_kernel, rows_count, cols_count, e...]
where the time goes in v3:
time: 58.9 us; the launch traced here: 58.7 us
  Pallas kernels  58 us (98%)
  between operations  0.65 us (1%)
    pallas_call x1, Pallas kernels, staged_local(): pl.pallas_call(functools.partial(staged_kernel, rows_count, cols_count, e...  48.5 us
    pallas_call x1, Pallas kernels, staged_local(): pl.pallas_call(functools.partial(finish_kernel, small), out_shape=[jax.Sh...  9.49 us

profile of v3, /device:TPU:0, one launch (start us, length us, event | category | flops | bytes accessed | tf_op | source)
XLA Modules:
  0.0 58.7 jit_solution(9454563525314514071)
XLA Ops:
  0.6 48.5 %shard_map.170 = (bf16[1024,13312]{1,0:T(8,128)(2,1)S(1)}, f32[1024,128]{1,0:T(8,128)S(1)}, f32[8,128]{1,0:T(8,128)S(1)}, f32[4,1024]{1,0:T(4,128)S(1)}, f32[4,1...) custom-call(s32[1,2]{1,0:T(1,128)} %tallies.1, ...), custom_call_target="tpu_custom_call" | custom-call | tf_op jit(solution)/shard_map/pallas_call | solution.py:924
  49.2 9.5 %shard_map.171 = (bf16[1024,13312]{1,0:T(8,128)(2,1)}, f32[8,128]{1,0:T(8,128)}, f32[4,1024]{1,0:T(4,128)}, f32[4,1024]{1,0:T(4,128)}, f32[4,1024]{1,0:T(4,128)}...) custom-call(bf16[1024,13312]{1,0:T(8,128)(2,1)S(1)} %get-tuple-element.25.merged, ...), custom_call_target="tpu_custom_call" | custom-call | tf_op jit(solution)/shard_map/pallas_call | solution.py:995

commit v4 on v3

--- a/solution.py
+++ b/solution.py
@@ -24,7 +24,7 @@
 fetch_lines = 64
 fetch_slots = 3
 decode_group = 32
-decode_width = 1664
+decode_width = 3328
 pass_width = 512
 pass_lines = 32
 out_lines = 64

time: 58.9 us -> 58.8 us (level)
  no operation moved by 1% of the time
where the time goes in v4:
time: 58.8 us; the launch traced here: 58.5 us
  Pallas kernels  57.8 us (98%)
  between operations  0.65 us (1%)
    pallas_call x1, Pallas kernels, staged_local(): pl.pallas_call(functools.partial(staged_kernel, rows_count, cols_count, e...  48.4 us
    pallas_call x1, Pallas kernels, staged_local(): pl.pallas_call(functools.partial(finish_kernel, small), out_shape=[jax.Sh...  9.44 us

profile of v4, /device:TPU:0, one launch (start us, length us, event | category | flops | bytes accessed | tf_op | source)
XLA Modules:
  0.0 58.5 jit_solution(6808044177927332771)
XLA Ops:
  0.6 48.4 %shard_map.170 = (bf16[1024,13312]{1,0:T(8,128)(2,1)S(1)}, f32[1024,128]{1,0:T(8,128)S(1)}, f32[8,128]{1,0:T(8,128)S(1)}, f32[4,1024]{1,0:T(4,128)S(1)}, f32[4,1...) custom-call(s32[1,2]{1,0:T(1,128)} %tallies.1, ...), custom_call_target="tpu_custom_call" | custom-call | tf_op jit(solution)/shard_map/pallas_call | solution.py:924
  49.1 9.4 %shard_map.171 = (bf16[1024,13312]{1,0:T(8,128)(2,1)}, f32[8,128]{1,0:T(8,128)}, f32[4,1024]{1,0:T(4,128)}, f32[4,1024]{1,0:T(4,128)}, f32[4,1024]{1,0:T(4,128)}...) custom-call(bf16[1024,13312]{1,0:T(8,128)(2,1)S(1)} %get-tuple-element.25.merged, ...), custom_call_target="tpu_custom_call" | custom-call | tf_op jit(solution)/shard_map/pallas_call | solution.py:995
